TPU v7x, 128 devices: a whole 4x4x4 slice. The times are simulated.
128 devices in a mesh: sector: 4 (over z_hi, core), op: 32 (over x, y, z_lo).
Axes of the slice: x: 4, y: 4, z: 4 (z_hi: 2, z_lo: 2; z = z_hi * 2 + z_lo), core: 2. Of those that a mesh axis runs over, the one named last changes fastest.
Arguments:
- wave: float32 [8, 768, 768], P('sector', 'op'), may hold values from -6 to 6
- onsite: float32 [8, 768, 768], P('sector', 'op'), may hold values from -2 to 2
- left_ops: float32 [8, 64, 768, 768], P('sector', 'op'), may hold values from -0.21875 to 0.21875
- right_ops: float32 [8, 64, 768, 768], P('sector', 'op'), may hold values from -0.02734375 to 0.02734375
- coupling: int32 [8, 64], P('sector', 'op'), may hold values from 0 to 2
Outputs:
- sigma: float32 [8, 768, 768], P('sector', 'op')
- correction: float32 [8, 768, 768], P('sector', 'op')
All inputs are finite; a program needn't handle non-finite values.
Results may differ from a plain program's by a relative error of at most 0.0001.
Values sent between devices are 32-bit elements; how exact they have to be, the bound alone decides.
A program may use at most 128 MiB of HBM per device.

v0:
```python
import functools

import jax
import jax.numpy as jnp
from jax import lax
from jax.sharding import Mesh
from jax.sharding import PartitionSpec as P

SECTOR = ("sector_0", "sector_1")
OP = ("op_0", "op_1", "op_2")
SECTOR_OP = ("sector_0", "sector_1", "op_0", "op_1", "op_2")


def shifted(value, axis, by):
    length = lax.axis_size(axis)
    return lax.ppermute(value, axis, [(i, (i + by) % length) for i in range(length)])


def side_by_side(arrays, axis, dim, along):
    both = jnp.concatenate(arrays, axis=along)
    result, at, gathered = (lax.all_gather(both, axis, axis=dim, tiled=True), 0, [])
    for a in arrays:
        gathered.append(lax.slice_in_dim(result, at, at + a.shape[along], axis=along))
        at += a.shape[along]
    return tuple(gathered)


def in_one_piece(arrays, axis, dim, along):
    ends, at = ([], 0)
    for a in arrays[:-1]:
        at += a.shape[along]
        ends.append(at)
    both = jnp.concatenate(arrays, axis=along)
    return tuple(
        jnp.split(lax.psum_scatter(both, axis, scatter_dimension=dim, tiled=True), ends, axis=along)
    )


def one_axis_at_a_time(value, axes):
    return functools.reduce(lax.psum, axes, value)


def on_device(wave, onsite, left_ops, right_ops, coupling):
    highest = lax.Precision.HIGHEST
    rows = wave.shape[1]
    width = wave.shape[2]
    ahead_rows = shifted(wave[0:1], SECTOR, -1)
    own_full, ahead_full = side_by_side((wave, ahead_rows), OP, 1, 0)
    following = jnp.concatenate([own_full[1:2], ahead_full], axis=0)
    left_fwd = jnp.einsum("jkac,jcb->jkab", left_ops, own_full, precision=highest)
    left_back = jnp.einsum("jkca,jcb->jkab", left_ops, following, precision=highest)
    weights = coupling.astype(jnp.float32)[:, :, None, None]
    forward = jnp.einsum("jkab,jkcb->jac", weights * left_fwd, right_ops, precision=highest)
    backward = jnp.einsum("jkab,jkbc->jac", weights * left_back, right_ops, precision=highest)
    partial_sums = jnp.stack([backward[0], backward[1] + forward[0]], axis=0)
    leaving = forward[1:2]
    summed, outgoing = in_one_piece((partial_sums, leaving), OP, 1, 0)
    arriving = shifted(outgoing, SECTOR, 1)
    sigma = onsite * wave + summed + jnp.concatenate([arriving, jnp.zeros_like(arriving)], axis=0)
    total = wave.shape[0] * rows * width * lax.axis_size(SECTOR) * lax.axis_size(OP)
    norm_sq, energy_sum = (
        one_axis_at_a_time(jnp.sum(wave * wave), SECTOR_OP),
        one_axis_at_a_time(jnp.sum(wave * sigma), SECTOR_OP),
    )
    energy = energy_sum / norm_sq
    gap = onsite - energy
    first = (sigma - energy * wave) * gap / jnp.maximum(gap * gap, 1.0)
    correlation, first_sq = (
        one_axis_at_a_time(jnp.sum(wave * first), SECTOR_OP),
        one_axis_at_a_time(jnp.sum(first * first), SECTOR_OP),
    )
    second = first - correlation / norm_sq * wave
    length_sq = first_sq - correlation * correlation / norm_sq
    correction = second * lax.rsqrt(length_sq / total + 1e-06)
    return (sigma, correction)


def solution(mesh):
    finer = Mesh(
        mesh.devices.reshape(2, 2, 4, 4, 2), ("sector_0", "sector_1", "op_0", "op_1", "op_2")
    )
    placed = (
        P(SECTOR, OP, None),
        P(SECTOR, OP, None),
        P(SECTOR, OP, None, None),
        P(SECTOR, OP, None, None),
        P(SECTOR, OP),
    )
    return jax.shard_map(
        on_device,
        mesh=finer,
        in_specs=placed,
        out_specs=(P(SECTOR, OP, None), P(SECTOR, OP, None)),
        check_vma=False,
    )
```

profile of v0, /device:TPU:1, one launch (start us, length us, event | category | flops | bytes accessed | tf_op | source)
XLA Modules:
  0.0 561.4 jit_solution(2225864658731541888)
XLA Ops:
  7.2 0.9 slice.22
  8.1 1.4 collective-permute-start
  9.5 5.6 %collective-permute-done = f32[1,24,768]{2,1,0:T(8,128)S(1)} collective-permute-done((f32[1,24,768]{2,1,0:T(8,128)S(1)}, f32[1,24,768]{2,1,0:T(8,128)S(1)}, u32[]{:S(2)}, u32[]{:S(2)}) %collective-permute-start) | collective-permute-done | bytes 73760 | tf_op jit(solution)/shard_map/ppermute | solution.py:16
  15.1 1.6 pad_maximum_fusion.1
  17.5 158.2 %all-gather.2.cloned.1.call-done = f32[3,768,768]{2,1,0:T(8,128)} async-done(((f32[3,24,768]{2,1,0:T(8,128)}), f32[3,768,768]{2,1,0:T(8,128)}) %all-gather.2.cloned.1.call-update) | async-done | bytes 7077904 | tf_op jit(solution)/shard_map/all_gather | solution.py:21
  175.6 27.4 %fusion.6 = f32[2,768,2,768]{1,3,2,0:T(8,128)} fusion(f32[2,2,768,768]{3,2,1,0:T(8,128)} %param.7, f32[3,768,768]{2,1,0:T(8,128)} %all-gather.2.cloned.1.call-done), kind=kOutput, calls=%fused_computation.8 | convolution fusion | flops 21743271936 | bytes 23592960 | tf_op jit(solution)/shard_map/jkac,jcb->jkab/dot_general | solution.py:50
  203.1 27.0 %fusion.13 = f32[2,768,768]{2,1,0:T(8,128)S(1)} fusion(f32[2,2,768,768]{3,2,1,0:T(8,128)} %param.8, f32[2,768,2,768]{1,3,2,0:T(8,128)} %fusion.6, f32[2,2]{1,0:T(2,128)S(1)} %convert_element_type.3), kind=kOutput, calls=%fused_computation.15 | convolution fusion | flops 21745631232 | bytes 23592976 | tf_op jit(solution)/shard_map/jkab,jkcb->jac/dot_general | solution.py:53
  230.2 27.6 %fusion.7 = f32[2,768,2,768]{1,3,2,0:T(8,128)} fusion(f32[2,2,768,768]{3,2,1,0:T(8,128)S(1)} %bitcast.31, f32[3,768,768]{2,1,0:T(8,128)S(1)} %bitcast.33), kind=kOutput, calls=%fused_computation.10 | convolution fusion | flops 21743271936 | bytes 23592960 | tf_op jit(solution)/shard_map/jkca,jcb->jkab/dot_general | solution.py:51
  257.7 27.0 %fusion.10 = f32[2,768,768]{2,1,0:T(8,128)S(1)} fusion(f32[2,2,768,768]{3,2,1,0:T(8,128)} %param.8, f32[2,768,2,768]{1,3,2,0:T(8,128)} %fusion.7, f32[2,2]{1,0:T(2,128)S(1)} %convert_element_type.3), kind=kOutput, calls=%fused_computation.14 | convolution fusion | flops 21745631232 | bytes 23592976 | tf_op jit(solution)/shard_map/jkab,jkbc->jac/dot_general | solution.py:54
  285.4 3.4 pad_maximum_fusion
  288.8 164.1 %reduce-scatter.2.cloned.1.call-done = f32[3,24,768]{2,1,0:T(8,128)} async-done(((f32[3,768,768]{2,1,0:T(8,128)}), f32[3,24,768]{2,1,0:T(8,128)}) %reduce-scatter.2.cloned.1.call-update) | async-done | bytes 221200 | tf_op jit(solution)/shard_map/reduce_scatter | solution.py:35
  453.8 26.8 %collective-permute-start.1 = (f32[1,24,768]{2,1,0:T(8,128)S(1)}, f32[1,24,768]{2,1,0:T(8,128)S(1)}, u32[]{:S(2)}, u32[]{:S(2)}) collective-permute-start(f32[1,24,768]{2,1,0:T(8,128)S(1)} %split.9), channel_id=1, source_target_pairs={{0,32},{32,64},{64,96},{96,0},{1,33},{33,65},{65,97},{97,1},{2,34}... | collective-permute-start | bytes 221192 | tf_op jit(solution)/shard_map/ppermute | solution.py:16
  480.6 1.4 collective-permute-done.1
  482.0 1.6 multiply_reduce_fusion.2
  483.6 5.9 %all-reduce.10 = (f32[]{:T(128)}, f32[]{:T(128)}) all-reduce(f32[]{:T(128)} %get-tuple-element.5, f32[]{:T(128)} %get-tuple-element.4), channel_id=1, replica_groups=mesh['sector_0'=2,'sector_1'=2,'op_0'=4,'op_1'=4,'op_2'=2] {'sector_0'}, use_global_device_ids=true, to_apply=%region_2.0 | all-reduce | flops 2 | bytes 16 | tf_op jit(solution)/shard_map/psum | solution.py:40
  489.5 4.7 all-reduce.8
  494.2 6.7 %all-reduce.4 = (f32[]{:T(128)}, f32[]{:T(128)}) all-reduce(f32[]{:T(128)} %get-tuple-element.20, f32[]{:T(128)} %get-tuple-element.21), channel_id=1, replica_groups=mesh['sector_0'=2,'sector_1'=2,'op_0'=4,'op_1'=4,'op_2'=2] {'op_0'}, use_global_device_ids=true, to_apply=%region_4.0 | all-reduce | flops 2 | bytes 16 | tf_op jit(solution)/shard_map/psum | solution.py:40
  501.0 7.2 %all-reduce.2 = (f32[]{:T(128)}, f32[]{:T(128)}) all-reduce(f32[]{:T(128)} %get-tuple-element.12, f32[]{:T(128)} %get-tuple-element.13), channel_id=1, replica_groups=mesh['sector_0'=2,'sector_1'=2,'op_0'=4,'op_1'=4,'op_2'=2] {'op_1'}, use_global_device_ids=true, to_apply=%region_5.0 | all-reduce | flops 2 | bytes 16 | tf_op jit(solution)/shard_map/psum | solution.py:40
  508.1 5.6 all-reduce.6
  515.7 6.0 %all-reduce.9 = (f32[]{:T(128)}, f32[]{:T(128)}) all-reduce(f32[]{:T(128)} %get-tuple-element.3, f32[]{:T(128)} %get-tuple-element.2), channel_id=1, replica_groups=mesh['sector_0'=2,'sector_1'=2,'op_0'=4,'op_1'=4,'op_2'=2] {'sector_0'}, use_global_device_ids=true, to_apply=%region_20.0 | all-reduce | flops 2 | bytes 16 | tf_op jit(solution)/shard_map/psum | solution.py:40
  521.7 9.2 %all-reduce.7 = (f32[]{:T(128)}, f32[]{:T(128)}) all-reduce(f32[]{:T(128)} %get-tuple-element.22, f32[]{:T(128)} %get-tuple-element.23), channel_id=1, replica_groups=mesh['sector_0'=2,'sector_1'=2,'op_0'=4,'op_1'=4,'op_2'=2] {'sector_1'}, use_global_device_ids=true, to_apply=%region_21.0 | all-reduce | flops 2 | bytes 16 | tf_op jit(solution)/shard_map/psum | solution.py:40
  530.9 6.8 %all-reduce.3 = (f32[]{:T(128)}, f32[]{:T(128)}) all-reduce(f32[]{:T(128)} %get-tuple-element.18, f32[]{:T(128)} %get-tuple-element.19), channel_id=1, replica_groups=mesh['sector_0'=2,'sector_1'=2,'op_0'=4,'op_1'=4,'op_2'=2] {'op_0'}, use_global_device_ids=true, to_apply=%region_22.0 | all-reduce | flops 2 | bytes 16 | tf_op jit(solution)/shard_map/psum | solution.py:40
  537.7 8.0 %all-reduce.1 = (f32[]{:T(128)}, f32[]{:T(128)}) all-reduce(f32[]{:T(128)} %get-tuple-element.10, f32[]{:T(128)} %get-tuple-element.11), channel_id=1, replica_groups=mesh['sector_0'=2,'sector_1'=2,'op_0'=4,'op_1'=4,'op_2'=2] {'op_1'}, use_global_device_ids=true, to_apply=%region_23.0 | all-reduce | flops 2 | bytes 16 | tf_op jit(solution)/shard_map/psum | solution.py:40
  545.7 4.5 all-reduce.5
  (27 shorter events, 3.9 us)
Async XLA Ops:
  7.2 168.5 %all-gather.2.cloned.1.call-start = ((), (), s32[]{:S(2)}) async-start(), calls=%async_computation.1 | async-start | bytes 7299072 | tf_op jit(solution)/shard_map/all_gather | solution.py:21
  8.1 7.0 %collective-permute-start = (f32[1,24,768]{2,1,0:T(8,128)S(1)}, f32[1,24,768]{2,1,0:T(8,128)S(1)}, u32[]{:S(2)}, u32[]{:S(2)}) collective-permute-start(f32[1,24,768]{2,1,0:T(8,128)S(1)} %slice.22), channel_id=1, source_target_pairs={{0,96},{32,0},{64,32},{96,64},{1,97},{33,1},{65,33},{97,65},{2,98}... | collective-permute-start | bytes 221192 | tf_op jit(solution)/shard_map/ppermute | solution.py:16
  16.7 436.2 %reduce-scatter.2.cloned.1.call-start = ((), (), s32[]{:S(2)}) async-start(), calls=%async_computation.2 | async-start | bytes 7299072 | tf_op jit(solution)/shard_map/reduce_scatter | solution.py:35
  175.6 54.5 %slice-start = ((s8[9437184]{0:T(1024)(128)(4,1)}), s8[4194304]{0:T(1024)(128)(4,1)S(1)}, s32[]{:S(2)}) async-start(s8[9437184]{0:T(1024)(128)(4,1)} %bitcast.30), calls=%async_computation.3 | async-start | bytes 8388608
  175.6 54.5 %slice-start.1 = ((s8[9437184]{0:T(1024)(128)(4,1)}), s8[4194304]{0:T(1024)(128)(4,1)S(1)}, s32[]{:S(2)}) async-start(s8[9437184]{0:T(1024)(128)(4,1)} %bitcast.30), calls=%async_computation.4 | async-start | bytes 8388608
  175.6 54.5 %slice-start.3 = ((s8[7077888]{0:T(1024)(128)(4,1)}), s8[4194304]{0:T(1024)(128)(4,1)S(1)}, s32[]{:S(2)}) async-start(s8[7077888]{0:T(1024)(128)(4,1)} %bitcast.32), calls=%async_computation.6 | async-start | bytes 8388608
  203.1 27.1 %slice-start.2 = ((s8[9437184]{0:T(1024)(128)(4,1)}), s8[1048576]{0:T(1024)(128)(4,1)S(1)}, s32[]{:S(2)}) async-start(s8[9437184]{0:T(1024)(128)(4,1)} %bitcast.30), calls=%async_computation.5 | async-start | bytes 2097152
  203.1 27.1 %slice-start.4 = ((s8[7077888]{0:T(1024)(128)(4,1)}), s8[2883584]{0:T(1024)(128)(4,1)S(1)}, s32[]{:S(2)}) async-start(s8[7077888]{0:T(1024)(128)(4,1)} %bitcast.32), calls=%async_computation.7 | async-start | bytes 5767168
  288.8 193.2 %copy-start = (f32[2,24,768]{2,1,0:T(8,128)S(1)}, f32[2,24,768]{2,1,0:T(8,128)}, u32[]{:S(2)}) copy-start(f32[2,24,768]{2,1,0:T(8,128)} %param.5) | copy-start | bytes 442372
  288.8 193.2 %copy-start.1 = (f32[2,24,768]{2,1,0:T(8,128)S(1)}, f32[2,24,768]{2,1,0:T(8,128)}, u32[]{:S(2)}) copy-start(f32[2,24,768]{2,1,0:T(8,128)} %param.6) | copy-start | bytes 442372
  453.8 28.2 %collective-permute-start.1 = (f32[1,24,768]{2,1,0:T(8,128)S(1)}, f32[1,24,768]{2,1,0:T(8,128)S(1)}, u32[]{:S(2)}, u32[]{:S(2)}) collective-permute-start(f32[1,24,768]{2,1,0:T(8,128)S(1)} %split.9), channel_id=1, source_target_pairs={{0,32},{32,64},{64,96},{96,0},{1,33},{33,65},{65,97},{97,1},{2,34}... | collective-permute-start | bytes 221192 | tf_op jit(solution)/shard_map/ppermute | solution.py:16
  483.6 70.9 %copy-start.2 = (f32[2,24,768]{2,1,0:T(8,128)}, f32[2,24,768]{2,1,0:T(8,128)S(1)}, u32[]{:S(2)}) copy-start(f32[2,24,768]{2,1,0:T(8,128)S(1)} %get-tuple-element.27) | copy-start | bytes 442372
Sparse Core Ops, SparseCore 0:
  16.9 158.7 all-gather.1
  289.0 163.9 reduce-scatter.1
where the time goes:
time: 566 us; the launch traced here: 561 us
  waiting for transfers between devices  329 us (58%)
  matrix products  109 us (19%)
  blocking collectives  64.5 us (11%)
  starting transfers between devices  28.2 us (5%)
  between operations  19.2 us (3%)
  other arithmetic  9.43 us (2%)
    reduce_scatter x1, waiting for transfers between devices, in_one_piece(): lax.psum_scatter(both, axis, scatter_dimension=dim, tiled=True)  164 us
    all_gather x1, waiting for transfers between devices, side_by_side(): lax.all_gather(both, axis, axis=dim, tiled=True)  158 us
    psum x10, blocking collectives, one_axis_at_a_time(): return functools.reduce(lax.psum, axes, value)  64.5 us
    ppermute x2, starting transfers between devices, shifted(): lax.ppermute(value, axis, [(i, (i + by) % length) for i in range(length)])  28.2 us
    dot_general x1, matrix products, on_device(): jnp.einsum('jkca,jcb->jkab', left_ops, following, precision=highest)  27.6 us
    dot_general x1, matrix products, on_device(): jnp.einsum('jkac,jcb->jkab', left_ops, own_full, precision=highest)  27.4 us
    dot_general x1, matrix products, on_device(): jnp.einsum('jkab,jkcb->jac', weights * left_fwd, right_ops, precision=hig...  27 us
    dot_general x1, matrix products, on_device(): jnp.einsum('jkab,jkbc->jac', weights * left_back, right_ops, precision=hi...  27 us
  transfers between devices with their start and end apart: 4, of which 4 were waited for; matrix products, arithmetic and copies ran while one was open for 0% of the time, Pallas kernels for 0%

commit v1 on v0

v1 whole, which is shorter than its diff:
```python
import functools

import jax
import jax.numpy as jnp
from jax import lax
from jax.experimental import pallas as pl
from jax.experimental.pallas import tpu as pltpu
from jax.sharding import Mesh
from jax.sharding import PartitionSpec as P

AXES = ("zh", "core", "x", "y", "zl")
SECTOR = ("zh", "core")
OP = ("x", "y", "zl")
MESH = pl.DeviceIdType.MESH
F32 = jnp.float32
BF16 = jnp.bfloat16
M = 768
RING = 4
SLAB = 48
ROWS = 24
HALF = 384
N_COPIES = 320


def split(v):
    hi = v.astype(BF16)
    return hi, (v - hi.astype(F32)).astype(BF16)


def dot3(a, b, dims):
    def one(p, q):
        return lax.dot_general(p, q, (dims, ((), ())), preferred_element_type=F32)

    return one(a[0], b[0]) + one(a[0], b[1]) + one(a[1], b[0])


NN = ((1,), (0,))
NT = ((1,), (1,))
TN = ((0,), (0,))


def fold(v):
    t = v.reshape(-1, 8, v.shape[-1]).sum(0)
    out = t[:, 0:128]
    for i in range(1, v.shape[-1] // 128):
        out = out + t[:, 128 * i : 128 * (i + 1)]
    return out


class Copies:
    def __init__(self, send, recv):
        self.send, self.recv, self.all = send, recv, []

    def new(self, src, dst, dev):
        c = Copy(self, len(self.all), src, dst, dev)
        assert c.i < N_COPIES
        self.all.append(c)
        return c


class Copy:
    def __init__(self, net, i, src, dst, dev):
        self.net, self.i, self.src, self.dst, self.dev = net, i, src, dst, dev

    def desc(self):
        return pltpu.make_async_remote_copy(
            src_ref=self.src(),
            dst_ref=self.dst(),
            send_sem=self.net.send.at[self.i],
            recv_sem=self.net.recv.at[self.i],
            device_id=self.dev,
            device_id_type=MESH,
        )

    def start(self):
        self.desc().start()

    def wait_recv(self):
        self.desc().wait_recv()

    def wait_send(self):
        self.desc().wait_send()


def kernel(
    wave, onsite, left, right, coup,
    sigma, corr,
    lh, ll, rh, rl, stage, W, uh, ul, Pb, pin, rbB, rbA, rbZ, red,
    load_sem, own_sem, send, recv,
):
    zh, core, x, y, zl = (lax.axis_index(a) for a in AXES)
    net = Copies(send, recv)
    d = 1 - 2 * core

    def at(px=None, py=None, pz=None, pc=None, ph=None):
        return (
            zh if ph is None else ph,
            core if pc is None else pc,
            x if px is None else px,
            y if py is None else py,
            zl if pz is None else pz,
        )

    def mod(v):
        return lax.rem(v + 8, RING)

    zprev = jnp.where(core == 0, 1 - zh, zh)
    zlprev = jnp.where(core == 0, 1 - zl, zl)
    prev_dev = (zprev, 1 - core, x, y, zlprev)
    znext = jnp.where(core == 1, 1 - zh, zh)
    zlnext = jnp.where(core == 1, 1 - zl, zl)
    next_dev = (znext, 1 - core, x, y, zlnext)

    barrier = pltpu.get_barrier_semaphore()
    peers = [at(px=mod(x + i)) for i in (1, 2, 3)] + [at(py=mod(y + i)) for i in (1, 2, 3)]
    cube = []
    for i in range(1, 8):
        cube.append(((zh + (i >> 2)) % 2, (core + ((i >> 1) & 1)) % 2, x, y, (zl + (i & 1)) % 2))
    peers += cube
    for p in peers:
        pl.semaphore_signal(barrier, inc=1, device_id=p, device_id_type=MESH)

    def load(i):
        src = left if i < 4 else right
        j = i % 4
        return pltpu.make_async_copy(src.at[j // 2, j % 2], stage.at[i % 3], load_sem.at[i % 3])

    order = [6, 7, 2, 3, 4, 5, 0, 1]
    loads = []
    for n, i in enumerate(order):
        src = left if i < 4 else right
        j = i % 4
        loads.append(pltpu.make_async_copy(src.at[j // 2, j % 2], stage.at[n % 3], load_sem.at[n % 3]))
    for n in range(3):
        loads[n].start()

    own = []
    for b in range(2):
        own.append(
            pltpu.make_async_copy(
                wave.at[b], W.at[b, x, y, pl.ds(pl.multiple_of(zl * ROWS, 8), ROWS), :], own_sem.at[b]
            )
        )
        own[-1].start()

    def split_op(n):
        i = order[n]
        hi_ref, lo_ref = (lh, ll) if i < 4 else (rh, rl)
        j = i % 4
        loads[n].wait()
        c = coup[j // 2, j % 2].astype(F32)

        def body(t, carry):
            rows = pl.ds(pl.multiple_of(t * 96, 16), 96)
            v = stage[n % 3, rows, :]
            if i < 4:
                v = v * c
            hi, lo = split(v)
            hi_ref[j, rows, :] = hi
            lo_ref[j, rows, :] = lo
            return carry

        lax.fori_loop(0, 8, body, 0)
        if n + 3 < 8:
            loads[n + 3].start()

    def lanes(h):
        return pl.ds(h * HALF, HALF)

    def spot(h, a, b):
        return (a, b) if h == 0 else (b, a)

    class Gather:
        def __init__(self, blk, h):
            self.blk, self.h = blk, h
            a, b = (x, y) if h == 0 else (y, x)
            self.a, self.b = a, b

            def slab(pa, pb):
                px, py = spot(h, pa, pb)
                return lambda: W.at[blk, px, py, :, lanes(h)]

            def dev(pa, pb):
                px, py = spot(h, pa, pb)
                return at(px=px, py=py)

            rows = pl.ds(pl.multiple_of(zl * ROWS, 8), ROWS)
            self.z = net.new(
                lambda: wave.at[blk, :, lanes(h)],
                lambda: W.at[blk, x, y, rows, lanes(h)],
                at(pz=1 - zl),
            )
            fa, ba = dev(mod(a + d), b), dev(mod(a - d), b)
            own_slab, from_back = slab(a, b), slab(mod(a - d), b)
            self.a1 = net.new(own_slab, own_slab, fa)
            self.a2 = net.new(own_slab, own_slab, ba)
            self.a3 = net.new(from_back, from_back, fa)
            fb, bb = dev(a, mod(b + d)), dev(a, mod(b - d))
            self.cols = []
            for o in (0, 1, 2, 3):
                pa = (a, mod(a - d), mod(a + d), mod(a + 2))[o]
                s, t = slab(pa, b), slab(pa, mod(b - d))
                self.cols.append((net.new(s, s, fb), net.new(s, s, bb), net.new(t, t, fb)))
            if blk == 0:
                def whole(pa):
                    if h == 0:
                        return (lambda: W.at[0, pa, :, :, lanes(0)]), (lambda: W.at[2, pa, :, :, lanes(0)])
                    return (lambda: W.at[0, :, pa, :, lanes(1)]), (lambda: W.at[2, :, pa, :, lanes(1)])

                self.ahead = []
                for o in range(4):
                    pa = (a, mod(a - d), mod(a + d), mod(a + 2))[o]
                    s, t = whole(pa)
                    self.ahead.append(net.new(s, t, prev_dev))

        def first(self):
            self.z.start()

        def second(self):
            self.z.wait_recv()
            self.a1.start()
            self.a2.start()
            self.spread(0)

        def spread(self, o):
            self.cols[o][0].start()
            self.cols[o][1].start()

        def third(self):
            self.a1.wait_recv()
            self.a3.start()
            self.spread(1)

        def fourth(self):
            self.a2.wait_recv()
            self.spread(2)

        def fifth(self):
            self.a3.wait_recv()
            self.spread(3)

        def relay(self, o):
            self.cols[o][0].wait_recv()
            self.cols[o][2].start()

        def finish(self, o):
            self.cols[o][1].wait_recv()
            self.cols[o][2].wait_recv()
            if self.blk == 0:
                self.ahead[o].start()

    g10, g11, g00, g01 = Gather(1, 0), Gather(1, 1), Gather(0, 0), Gather(0, 1)

    class Scatter:
        def __init__(self, blk, h):
            self.blk, self.h = blk, h
            a, b = (x, y) if h == 0 else (y, x)
            self.a, self.b = a, b
            u = blk * 2 + h

            def slab(pa, pb):
                px, py = spot(h, pa, pb)
                return lambda: Pb.at[blk, px, py, :, lanes(h)]

            def dev(pa, pb):
                px, py = spot(h, pa, pb)
                return at(px=px, py=py)

            self.slab = slab

            def buf(o, s):
                return lambda: rbB.at[u, o, s]

            def bufa(s):
                return lambda: rbA.at[u, s]

            self.rb, self.ra = (lambda o, s: rbB.at[u, o, s]), (lambda s: rbA.at[u, s])
            fb, bb = dev(a, mod(b + d)), dev(a, mod(b - d))
            self.cols = []
            for o in range(4):
                self.cols.append(
                    (
                        net.new(slab(o, mod(b + 2)), buf(o, 0), fb),
                        net.new(slab(o, mod(b - d)), buf(o, 1), bb),
                        net.new(slab(o, mod(b + d)), buf(o, 2), fb),
                    )
                )
            fa, ba = dev(mod(a + d), b), dev(mod(a - d), b)
            self.ring = (
                net.new(slab(mod(a + 2), b), bufa(0), fa),
                net.new(slab(mod(a - d), b), bufa(1), ba),
                net.new(slab(mod(a + d), b), bufa(2), fa),
            )
            other = pl.ds(pl.multiple_of((1 - zl) * ROWS, 8), ROWS)
            self.z = net.new(
                lambda: Pb.at[blk, x, y, other, lanes(h)], lambda: rbZ.at[blk, :, lanes(h)], at(pz=1 - zl)
            )

        def first(self, o):
            self.cols[o][0].start()
            self.cols[o][1].start()

        def relay(self, o):
            c = self.cols[o]
            c[0].wait_recv()
            s = self.slab(o, mod(self.b + d))()
            s[...] = s[...] + self.rb(o, 0)[...]
            c[2].start()

        def land(self, o):
            c = self.cols[o]
            c[1].wait_recv()
            c[2].wait_recv()
            s = self.slab(o, self.b)()
            s[...] = s[...] + self.rb(o, 1)[...] + self.rb(o, 2)[...]

        def ring_first(self):
            self.ring[0].start()
            self.ring[1].start()

        def ring_relay(self):
            self.ring[0].wait_recv()
            s = self.slab(mod(self.a + d), self.b)()
            s[...] = s[...] + self.ra(0)[...]
            self.ring[2].start()

        def ring_land(self):
            self.ring[1].wait_recv()
            self.ring[2].wait_recv()
            s = self.slab(self.a, self.b)()
            s[...] = s[...] + self.ra(1)[...] + self.ra(2)[...]
            self.z.start()

    s10, s11, s00, s01 = Scatter(1, 0), Scatter(1, 1), Scatter(0, 0), Scatter(0, 1)
    give = [
        net.new(
            lambda m=m: Pb.at[2, pl.ds(2 * m, 2)], lambda m=m: pin.at[pl.ds(2 * m, 2)], next_dev
        )
        for m in range(2)
    ]

    class Total:
        def __init__(self, n):
            self.n = n
            base = n * 16
            self.px, self.py, self.pz = (
                lambda i: red.at[base + i],
                lambda i: red.at[base + 4 + i],
                lambda i: red.at[base + 8 + i],
            )
            self.me = zh * 4 + core * 2 + zl
            self.cx = [net.new(lambda: self.px(x), lambda: self.px(x), at(px=mod(x + i))) for i in (1, 2, 3)]
            self.cy = [net.new(lambda: self.py(y), lambda: self.py(y), at(py=mod(y + i))) for i in (1, 2, 3)]
            self.cz = [net.new(lambda: self.pz(self.me), lambda: self.pz(self.me), p) for p in cube]

        def one(self, pair):
            r = self.px(x)
            r[...] = pair
            for c in self.cx:
                c.start()

        def two(self):
            for c in self.cx:
                c.wait_recv()
            s = self.px(0)[...]
            for i in range(1, 4):
                s = s + self.px(i)[...]
            r = self.py(y)
            r[...] = s
            for c in self.cy:
                c.start()

        def three(self):
            for c in self.cy:
                c.wait_recv()
            s = self.py(0)[...]
            for i in range(1, 4):
                s = s + self.py(i)[...]
            r = self.pz(self.me)
            r[...] = s
            for c in self.cz:
                c.start()

        def four(self):
            for c in self.cz:
                c.wait_recv()
            s = self.pz(0)[...]
            for i in range(1, 8):
                s = s + self.pz(i)[...]
            return jnp.sum(s[0], keepdims=True), jnp.sum(s[1], keepdims=True)

    def stage1(blk, j, transposed, hooks):
        def body(i, carry):
            for n, hook in enumerate(hooks):
                pl.when(i == n)(hook)
            m = lax.rem(i, 2)
            k = lax.div(i, 2)
            w = split(W[blk, pl.ds(2 * m, 2)].reshape(HALF, M))
            r = (rh[2 * j + k], rl[2 * j + k])
            u = split(dot3(w, r, NT if transposed else NN))
            rows = pl.ds(pl.multiple_of(m * HALF, HALF), HALF)
            uh[k, rows, :] = u[0]
            ul[k, rows, :] = u[1]
            return carry

        lax.fori_loop(0, 4, body, 0)

    def stage2(j, transposed, hooks, put):
        def body(m, carry):
            for n, hook in enumerate(hooks):
                pl.when(m == n)(hook)
            cut = pl.ds(pl.multiple_of(m * HALF, HALF), HALF)
            total = None
            for k in range(2):
                if transposed:
                    a = (lh[2 * j + k, :, cut], ll[2 * j + k, :, cut])
                else:
                    a = (lh[2 * j + k, cut, :], ll[2 * j + k, cut, :])
                t = dot3(a, (uh[k], ul[k]), TN if transposed else NN)
                total = t if total is None else total + t
            put(m, total.reshape(2, RING, SLAB, M))
            return carry

        lax.fori_loop(0, 2, body, 0)

    def put_to(blk):
        def put(m, v):
            Pb[blk, pl.ds(2 * m, 2)] = v

        return put

    def add_to(blk):
        def put(m, v):
            s = pl.ds(2 * m, 2)
            Pb[blk, s] = Pb[blk, s] + v

        return put

    def put_with_pin(m, v):
        s = pl.ds(2 * m, 2)
        Pb[0, s] = pin[s] + v

    def inner(wblk, pblk):
        def body(i, acc):
            return acc + fold((W[wblk, i] * Pb[pblk, i]).reshape(RING * SLAB, M))

        return lax.fori_loop(0, 4, body, jnp.zeros((8, 128), F32))

    pl.semaphore_wait(barrier, len(peers))
    for g in (g10, g11, g00, g01):
        g.first()
    split_op(0)
    own[0].wait()
    own[1].wait()
    g10.second()
    g11.second()
    split_op(1)
    for s in ("third", "fourth"):
        getattr(g10, s)()
        getattr(g11, s)()
    split_op(2)
    g10.relay(0)
    g11.relay(0)
    g10.fifth()
    g11.fifth()
    g00.second()
    g01.second()
    split_op(3)
    for o in (1, 2, 3):
        g10.relay(o)
        g11.relay(o)
    split_op(4)
    for s in ("third", "fourth"):
        getattr(g00, s)()
        getattr(g01, s)()
    split_op(5)
    g00.relay(0)
    g01.relay(0)
    g00.fifth()
    g01.fifth()
    for o in (0, 1, 2, 3):
        g10.finish(o)
        g11.finish(o)

    def both(fn):
        return lambda: (fn(g00), fn(g01), None)[2]

    stage1(
        1, 1, True,
        [both(lambda g: g.relay(1)), both(lambda g: g.relay(2)), both(lambda g: g.relay(3)), both(lambda g: g.finish(0))],
    )
    stage2(1, False, [both(lambda g: g.finish(1)), both(lambda g: g.finish(2))], put_to(2))
    give[0].start()
    give[1].start()
    g00.finish(3)
    g01.finish(3)
    split_op(6)
    split_op(7)
    stage1(0, 0, True, [])
    stage2(0, False, [], put_to(1))
    for g in (g00, g01):
        for o in range(4):
            g.ahead[o].wait_recv()
    w01 = [wave[b] for b in range(2)]
    pp = fold(w01[0] * w01[0]) + fold(w01[1] * w01[1])
    ps = fold(onsite[0] * w01[0] * w01[0]) + fold(onsite[1] * w01[1] * w01[1])
    ps = ps + 2.0 * (inner(1, 1) + inner(2, 2))
    t0, t1 = Total(0), Total(1)
    t0.one(jnp.stack([pp, ps]))
    stage1(2, 1, False, [lambda: None, t0.two])
    stage2(1, True, [t0.three], add_to(1))

    pair1 = (s10, s11)
    for s in pair1:
        for o in range(4):
            s.first(o)

    def on(pair, fn):
        return lambda: (fn(pair[0]), fn(pair[1]), None)[2]

    stage1(
        1, 0, False,
        [
            lambda: None,
            on(pair1, lambda s: (s.relay(0), s.relay(1))),
            on(pair1, lambda s: (s.relay(2), s.relay(3))),
            lambda: None,
        ],
    )
    for g in give:
        g.wait_recv()
    for s in pair1:
        for o in range(4):
            s.land(o)
        s.ring_first()
    stage2(0, True, [lambda: None, on(pair1, lambda s: s.ring_relay())], put_with_pin)
    pair0 = (s00, s01)
    for s in pair0:
        for o in range(4):
            s.first(o)
    for s in pair1:
        s.ring_land()
    for o in range(4):
        for s in pair0:
            s.relay(o)
    norm_sq, energy_sum = t0.four()
    energy = energy_sum / norm_sq
    for o in range(4):
        for s in pair0:
            s.land(o)
    for s in pair0:
        s.ring_first()
    for s in pair0:
        s.ring_relay()
    for s in pair0:
        s.ring_land()
    mine = pl.ds(pl.multiple_of(zl * ROWS, 8), ROWS)
    pt = jnp.zeros((8, 128), F32)
    tt = jnp.zeros((8, 128), F32)
    for b in (1, 0):
        for s in (s10, s11) if b == 1 else pair0:
            s.z.wait_recv()
        w = wave[b]
        sig = onsite[b] * w + Pb[b, x, y, mine, :] + rbZ[b]
        sigma[b] = sig
        gap = onsite[b] - energy
        first = (sig - energy * w) * gap / jnp.maximum(gap * gap, 1.0)
        corr[b] = first
        pt = pt + fold(w * first)
        tt = tt + fold(first * first)
    t1.one(jnp.stack([pt, tt]))
    t1.two()
    t1.three()
    correlation, first_sq = t1.four()
    ratio = correlation / norm_sq
    length_sq = first_sq - correlation * ratio
    scale = lax.rsqrt(length_sq / float(8 * M * M) + 1e-06)
    for b in range(2):
        corr[b] = (corr[b] - ratio * wave[b]) * scale
    for c in net.all:
        c.wait_send()


def solution(mesh):
    finer = Mesh(mesh.devices.reshape(2, 2, 4, 4, 2), AXES)
    block = P(SECTOR, OP, None)
    ops = P(SECTOR, OP, None, None)

    def step(wave, onsite, left, right, coupling):
        vm = pl.BlockSpec(memory_space=pltpu.VMEM)
        anyw = pl.BlockSpec(memory_space=pl.ANY)
        shape = jax.ShapeDtypeStruct((2, ROWS, M), F32)
        return pl.pallas_call(
            kernel,
            out_shape=(shape, shape),
            in_specs=[vm, vm, anyw, anyw, pl.BlockSpec(memory_space=pltpu.SMEM)],
            out_specs=(vm, vm),
            scratch_shapes=[
                pltpu.VMEM((4, M, M), BF16),
                pltpu.VMEM((4, M, M), BF16),
                pltpu.VMEM((4, M, M), BF16),
                pltpu.VMEM((4, M, M), BF16),
                pltpu.VMEM((3, M, M), F32),
                pltpu.VMEM((3, RING, RING, SLAB, M), F32),
                pltpu.VMEM((2, M, M), BF16),
                pltpu.VMEM((2, M, M), BF16),
                pltpu.VMEM((3, RING, RING, SLAB, M), F32),
                pltpu.VMEM((RING, RING, SLAB, M), F32),
                pltpu.VMEM((4, 4, 3, SLAB, HALF), F32),
                pltpu.VMEM((4, 3, SLAB, HALF), F32),
                pltpu.VMEM((2, ROWS, M), F32),
                pltpu.VMEM((32, 2, 8, 128), F32),
                pltpu.SemaphoreType.DMA((3,)),
                pltpu.SemaphoreType.DMA((2,)),
                pltpu.SemaphoreType.DMA((N_COPIES,)),
                pltpu.SemaphoreType.DMA((N_COPIES,)),
            ],
            compiler_params=pltpu.CompilerParams(
                collective_id=0, has_side_effects=True, vmem_limit_bytes=67043328
            ),
        )(wave, onsite, left, right, coupling)

    return jax.shard_map(
        step,
        mesh=finer,
        in_specs=(block, block, ops, ops, P(SECTOR, OP)),
        out_specs=(block, block),
        check_vma=False,
    )
```

time: 566 us -> 154 us (0.27)
  waiting for transfers between devices: 329 us -> 0 us
  Pallas kernels: 0 us -> 150 us
  matrix products: 109 us -> 0 us
  blocking collectives: 64.5 us -> 0 us
  starting transfers between devices: 28.2 us -> 0 us
  between operations: 19.2 us -> 0.64 us
  other arithmetic: 9.43 us -> 0 us
    reduce_scatter x1 -> x0, waiting for transfers between devices: 164 us -> none  [in_one_piece(): lax.psum_scatter(both, axis, scatter_dimension=dim, tiled=True)]
    all_gather x1 -> x0, waiting for transfers between devices: 158 us -> none  [side_by_side(): lax.all_gather(both, axis, axis=dim, tiled=True)]
    pallas_call x0 -> x1, Pallas kernels: none -> 150 us  [step(): pl.pallas_call(kernel, out_shape=(shape, shape), in_specs=[vm, vm, anyw,...]
    dot_general x4 -> x0, matrix products: 109 us -> none  [the longest x1 27.6 us: on_device(): jnp.einsum('jkca,jcb->jkab', left_ops, following, precision=highest)]
    psum x10 -> x0, blocking collectives: 64.5 us -> none  [one_axis_at_a_time(): return functools.reduce(lax.psum, axes, value)]
    ppermute x2 -> x0, starting transfers between devices: 28.2 us -> none  [shifted(): lax.ppermute(value, axis, [(i, (i + by) % length) for i in range(length)])]
    ppermute x2 -> x0, waiting for transfers between devices: 7.04 us -> none  [shifted(): lax.ppermute(value, axis, [(i, (i + by) % length) for i in range(length)])]
  transfers between devices with their start and end apart: 4 -> 0, of which waited for: 4 -> 0; matrix products, arithmetic and copies ran while one was open for 0% -> 0% of each run, Pallas kernels for 0% -> 0%
where the time goes in v1:
time: 154 us
  Pallas kernels  150 us (97%)
  local copies, waits for them, and re-layouts  3.16 us (2%)
    pallas_call x1, Pallas kernels, step(): pl.pallas_call(kernel, out_shape=(shape, shape), in_specs=[vm, vm, anyw,...  150 us
    unnamed x2, local copies, waits for them, and re-layouts  3.16 us

profile of v1, /device:TPU:1, one launch (start us, length us, event | category | flops | bytes accessed | tf_op | source)
XLA Modules:
  0.0 153.8 jit_solution(17566906897899853955)
XLA Ops:
  0.6 150.0 %shard_map.68 = (f32[2,24,768]{2,1,0:T(8,128)}, f32[2,24,768]{2,1,0:T(8,128)}) custom-call(f32[2,24,768]{2,1,0:T(8,128)} %wave.1, f32[2,24,768]{2,1,0:T(8,128)} %onsite.1, f32[2,2,768,768]{3,2,1,0:T(8,128)} %left.1, f32[2,2,768,768]{3,2,1,0:T(8,128)} %right.1, s32[2,2]{1,0:T(2,128)} %coup.1), custom_call_target="tpu_custom_call" | custom-call | tf_op jit(solution)/shard_map/pallas_call | solution.py:593
  150.6 1.6 %copy.9 = f32[2,24,768]{2,1,0:T(8,128)} copy(f32[2,24,768]{2,1,0:T(8,128)} %get-tuple-element.4) | data formatting | bytes 294912
  152.2 1.6 %copy.10 = f32[2,24,768]{2,1,0:T(8,128)} copy(f32[2,24,768]{2,1,0:T(8,128)} %get-tuple-element.5) | data formatting | bytes 294912

commit v2 on v1

v2 whole, which is shorter than its diff:
```python
import functools

import jax
import jax.numpy as jnp
from jax import lax
from jax.experimental import pallas as pl
from jax.experimental.pallas import tpu as pltpu
from jax.sharding import Mesh
from jax.sharding import PartitionSpec as P

AXES = ("zh", "core", "x", "y", "zl")
SECTOR = ("zh", "core")
OP = ("x", "y", "zl")
MESH = pl.DeviceIdType.MESH
F32 = jnp.float32
BF16 = jnp.bfloat16
M = 768
RING = 4
SLAB = 48
ROWS = 24
HALF = 384
N_SEND = 7
N_RECV = 112


def split(v):
    hi = v.astype(BF16)
    return hi, (v - hi.astype(F32)).astype(BF16)


def dot3(a, b, dims):
    def one(p, q):
        return lax.dot_general(p, q, (dims, ((), ())), preferred_element_type=F32)

    return one(a[0], b[0]) + one(a[0], b[1]) + one(a[1], b[0])


NN = ((1,), (0,))
NT = ((1,), (1,))
TN = ((0,), (0,))


def fold(v):
    t = v.reshape(-1, 8, v.shape[-1]).sum(0)
    out = t[:, 0:128]
    for i in range(1, v.shape[-1] // 128):
        out = out + t[:, 128 * i : 128 * (i + 1)]
    return out


class Copies:
    def __init__(self, send, recv):
        self.send, self.recv, self.got = send, recv, 0

    def new_recv(self):
        assert self.got < N_RECV
        self.got += 1
        return self.got - 1

    def new(self, src, dst, dev, group, got=None, sends=None, gets=None):
        return Copy(self, src, dst, dev, group, self.new_recv() if got is None else got, sends, gets)


class Copy:
    def __init__(self, net, src, dst, dev, group, got, sends, gets):
        self.net, self.src, self.dst, self.dev = net, src, dst, dev
        self.group, self.got, self.sends, self.gets = group, got, sends, gets

    def desc(self):
        return pltpu.make_async_remote_copy(
            src_ref=self.src(),
            dst_ref=self.dst(),
            send_sem=self.net.send.at[self.group],
            recv_sem=self.net.recv.at[self.got],
            device_id=self.dev,
            device_id_type=MESH,
        )

    def under(self, cond, act):
        if cond is None:
            act(self.desc())
        else:
            pl.when(cond)(lambda: act(self.desc()))

    def start(self):
        self.under(self.sends, lambda c: c.start())

    def wait_recv(self):
        self.under(self.gets, lambda c: c.wait_recv())


def wait_bytes(sem, like):
    pltpu.make_async_copy(like, like, sem).wait()


def kernel(
    wave, onsite, left, right, coup,
    psum_out, first_out, ratio_out, scale_out,
    lh, ll, rh, rl, stage, W, uh, ul, Pb, pin, zin, rbB, rbZ, red, wv, on_, ob,
    load_sem, own_sem, in_sem, out_sem, send, recv,
):
    zh, core, x, y, zl = (lax.axis_index(a) for a in AXES)
    net = Copies(send, recv)
    d = 1 - 2 * core

    def at(px=None, py=None, pz=None):
        return (zh, core, x if px is None else px, y if py is None else py, zl if pz is None else pz)

    def mod(v):
        return lax.rem(v + 8, RING)

    zprev = jnp.where(core == 0, 1 - zh, zh)
    zlprev = jnp.where(core == 0, 1 - zl, zl)
    prev_dev = (zprev, 1 - core, x, y, zlprev)
    znext = jnp.where(core == 1, 1 - zh, zh)
    zlnext = jnp.where(core == 1, 1 - zl, zl)
    next_dev = (znext, 1 - core, x, y, zlnext)

    barrier = pltpu.get_barrier_semaphore()
    peers = []
    for i in (1, 2, 3):
        for o in (0, 1):
            peers.append(at(px=mod(x + i), pz=(zl + o) % 2))
            peers.append(at(py=mod(y + i), pz=(zl + o) % 2))
    cube = []
    for i in range(1, 8):
        cube.append(((zh + (i >> 2)) % 2, (core + ((i >> 1) & 1)) % 2, x, y, (zl + (i & 1)) % 2))
    for i in (1, 2, 3):
        for k in (1, 2, 3):
            peers.append(at(px=mod(x + i), py=mod(y + k)))
    peers += cube
    for p in peers:
        pl.semaphore_signal(barrier, inc=1, device_id=p, device_id_type=MESH)

    own = []
    for b in range(2):
        own.append(
            pltpu.make_async_copy(
                wave.at[b], W.at[b, x, y, pl.ds(pl.multiple_of(zl * ROWS, 8), ROWS), :], own_sem.at[b]
            )
        )
        own[-1].start()

    order = [4, 5, 0, 1, 6, 7, 2, 3]
    loads = []
    for n, i in enumerate(order):
        src = left if i < 4 else right
        j = i % 4
        loads.append(pltpu.make_async_copy(src.at[j // 2, j % 2], stage.at[n % 3], load_sem.at[n % 3]))
    for n in range(3):
        loads[n].start()
    fetch = [
        pltpu.make_async_copy(wave, wv, in_sem.at[0]),
        pltpu.make_async_copy(onsite, on_, in_sem.at[1]),
    ]
    for c in fetch:
        c.start()

    def split_op(n):
        i = order[n]
        hi_ref, lo_ref = (lh, ll) if i < 4 else (rh, rl)
        j = i % 4
        loads[n].wait()
        c = coup[j // 2, j % 2].astype(F32)

        def body(t, carry):
            rows = pl.ds(pl.multiple_of(t * 96, 16), 96)
            v = stage[n % 3, rows, :]
            if i < 4:
                v = v * c
            hi, lo = split(v)
            hi_ref[j, rows, :] = hi
            lo_ref[j, rows, :] = lo
            return carry

        lax.fori_loop(0, 8, body, 0)
        if n + 3 < 8:
            loads[n + 3].start()

    def lanes(h):
        return pl.ds(h * HALF, HALF)

    def spot(h, a, b):
        return (a, b) if h == 0 else (b, a)

    def rows_of(z):
        return pl.ds(pl.multiple_of(z * ROWS, 8), ROWS)

    ahead_got = net.new_recv()

    class Gather:
        def __init__(self, blk, h):
            self.blk, self.h = blk, h
            a, b = (x, y) if h == 0 else (y, x)

            def slab(pa, pb):
                px, py = spot(h, pa, pb)
                return lambda: W.at[blk, px, py, :, lanes(h)]

            def dev(pa, pb, z=None):
                px, py = spot(h, pa, pb)
                return at(px=px, py=py, pz=z)

            self.near, self.got = {}, []
            for i in range(4):
                self.got.append(net.new_recv())
                for o in (1, 0):
                    if (i, o) != (0, 0):
                        self.near[i, o] = net.new(
                            lambda: wave.at[blk, :, lanes(h)],
                            lambda: W.at[blk, x, y, rows_of(zl), lanes(h)],
                            dev(mod(a + i), b, (zl + o) % 2),
                            0,
                            self.got[i],
                        )
            fb, bb = dev(a, mod(b + d)), dev(a, mod(b - d))
            self.cols, self.ahead = [], []
            for o in range(4):
                pa = mod(a - o)
                s, t = slab(pa, b), slab(pa, mod(b - d))
                self.cols.append((net.new(s, s, fb, 1), net.new(s, s, bb, 1), net.new(t, t, fb, 1)))
                if blk == 0:
                    on = []
                    for pb in (b, mod(b - d), mod(b + d), mod(b + 2)):
                        px, py = spot(h, pa, pb)

                        def src(px=px, py=py):
                            return W.at[0, px, py, :, lanes(h)]

                        def dst(px=px, py=py):
                            return W.at[2, px, py, :, lanes(h)]

                        on.append(net.new(src, dst, prev_dev, 2, ahead_got))
                    self.ahead.append(on)

        def pass_on(self, o, s):
            if self.blk == 0:
                self.ahead[o][s].start()

        def spread(self, o):
            if o == 0:
                self.near[0, 1].wait_recv()
            else:
                wait_bytes(recv.at[self.got[o]], rbB.at[0, 0, 0])
            self.cols[o][0].start()
            self.cols[o][1].start()
            self.pass_on(o, 0)

        def relay(self, o):
            self.cols[o][0].wait_recv()
            self.cols[o][2].start()
            self.pass_on(o, 1)

        def finish(self, o):
            self.cols[o][1].wait_recv()
            self.pass_on(o, 2)
            self.cols[o][2].wait_recv()
            self.pass_on(o, 3)

    g10, g11, g00, g01 = Gather(1, 0), Gather(1, 1), Gather(0, 0), Gather(0, 1)

    def step1(pair):
        for i in (0, 1, 3, 2):
            for o in (1, 0):
                if (i, o) != (0, 0):
                    for g in pair:
                        g.near[i, o].start()

    class Scatter:
        def __init__(self, blk, h):
            self.blk, self.h = blk, h
            a, b = (x, y) if h == 0 else (y, x)
            self.a, self.b = a, b
            u = blk * 2 + h
            self.u = u

            def slab(pa, pb):
                px, py = spot(h, pa, pb)
                return lambda: Pb.at[blk, px, py, :, lanes(h)]

            def dev(pa, pb, z=None):
                px, py = spot(h, pa, pb)
                return at(px=px, py=py, pz=z)

            self.slab = slab

            def buf(o, s):
                return lambda: rbB.at[u, o, s]

            self.rb = lambda o, s: rbB.at[u, o, s]
            fb, bb = dev(a, mod(b + d)), dev(a, mod(b - d))
            self.cols = []
            for o in range(4):
                both = net.new_recv()
                self.cols.append(
                    (
                        net.new(slab(o, mod(b + 2)), buf(o, 0), fb, 3),
                        net.new(slab(o, mod(b - d)), buf(o, 1), bb, 3, both),
                        net.new(slab(o, mod(b + d)), buf(o, 2), fb, 3, both),
                        both,
                    )
                )
            self.near, self.got = [], net.new_recv()
            for i in (2, 1, 3, 0):
                for o in (1, 0):
                    if (i, o) != (0, 0):
                        px, py = spot(h, mod(a + i), b)
                        z = (zl + o) % 2

                        def src(px=px, py=py, z=z):
                            return Pb.at[blk, px, py, rows_of(z), lanes(h)]

                        def dst(k=i * 2 + o):
                            return rbZ.at[u, k]

                        self.near.append(net.new(src, dst, dev(mod(a + i), b, z), 4, self.got))

        def first(self, o, half=None):
            c = self.cols[o]
            if half is None or self.h == 0:
                if half is None or o // 2 == half:
                    c[0].start()
                    c[1].start()
            else:
                pl.when(lax.div(mod(self.b + 2), 2) == half)(c[0].start)
                pl.when(lax.div(mod(self.b - d), 2) == half)(c[1].start)

        def relay(self, o):
            c = self.cols[o]
            c[0].wait_recv()
            s = self.slab(o, mod(self.b + d))()
            s[...] = s[...] + self.rb(o, 0)[...]
            c[2].start()

        def land(self, o):
            c = self.cols[o]
            wait_bytes(recv.at[c[3]], rbB.at[self.u, o, pl.ds(1, 2)])
            s = self.slab(o, self.b)()
            s[...] = s[...] + self.rb(o, 1)[...] + self.rb(o, 2)[...]

        def last(self):
            for c in self.near:
                c.start()

        def result(self):
            wait_bytes(recv.at[self.got], rbZ.at[self.u, pl.ds(1, 7)])
            t = Pb[self.blk, x, y, rows_of(zl), lanes(self.h)]
            for k in range(1, 8):
                t = t + rbZ[self.u, k]
            return t

    s10, s11, s00, s01 = Scatter(1, 0), Scatter(1, 1), Scatter(0, 0), Scatter(0, 1)

    ex = [
        net.new((lambda q=q: Pb.at[2, (1 - zl) * 2 + q]), (lambda q=q: zin.at[q]), at(pz=1 - zl), 5, sends=core == 1)
        for q in range(2)
    ]
    pin_got = net.new_recv()
    far = [
        net.new((lambda q=q: Pb.at[2, zl * 2 + q]), (lambda q=q: pin.at[zl * 2 + q]), next_dev, 5, pin_got)
        for q in range(2)
    ]
    chip = [
        net.new((lambda q=q: Pb.at[2, q]), (lambda q=q: pin.at[q]), next_dev, 5, pin_got, sends=core == 0)
        for q in range(4)
    ]

    def take_pin():
        pl.when(core == 1)(lambda: wait_bytes(recv.at[pin_got], pin))
        pl.when(core == 0)(lambda: wait_bytes(recv.at[pin_got], pin.at[pl.ds(0, 2)]))

    def give():
        for c in ex + chip:
            c.start()

    def fold_pair(q):
        @pl.when(core == 1)
        def _():
            ex[q].desc().wait_recv()
            i = zl * 2 + q
            Pb[2, i] = Pb[2, i] + zin[q]
            far[q].desc().start()

    plane = []
    for i in range(RING):
        for k in range(RING):
            if (i, k) != (0, 0):
                plane.append(at(px=mod(x + i), py=mod(y + k)))
    GX = ([at(px=mod(x + i)) for i in (1, 2, 3)], x)
    GY = ([at(py=mod(y + i)) for i in (1, 2, 3)], y)
    GC = (cube, zh * 4 + core * 2 + zl)
    GP = (plane, x * RING + y)

    class Total:
        def __init__(self, base, groups):
            self.stages = []
            for devs, me in groups:
                n = len(devs) + 1
                got = net.new_recv()

                def spot_of(base=base, me=me):
                    return red.at[base + me]

                copies = [net.new(spot_of, spot_of, p, 6, got) for p in devs]
                self.stages.append((base, n, spot_of, copies, got))
                base += n
            self.end = base

        def put(self, k, pair):
            _, _, spot_of, copies, _ = self.stages[k]
            r = spot_of()
            r[...] = pair
            for c in copies:
                c.start()

        def get(self, k):
            base, n, _, copies, got = self.stages[k]
            wait_bytes(recv.at[got], red.at[pl.ds(0, n - 1)])
            s = red[base]
            for i in range(1, n):
                s = s + red[base + i]
            return s

        def step(self, k):
            self.put(k + 1, self.get(k))

        def done(self):
            s = self.get(len(self.stages) - 1)
            return jnp.sum(s[0], keepdims=True), jnp.sum(s[1], keepdims=True)

    def stage1(blk, j, transposed, hooks):
        def body(i, carry):
            for n, hook in enumerate(hooks):
                pl.when(i == n)(hook)
            m = lax.rem(i, 2)
            k = lax.div(i, 2)
            w = split(W[blk, pl.ds(2 * m, 2)].reshape(HALF, M))
            r = (rh[2 * j + k], rl[2 * j + k])
            u = split(dot3(w, r, NT if transposed else NN))
            rows = pl.ds(pl.multiple_of(m * HALF, HALF), HALF)
            uh[k, rows, :] = u[0]
            ul[k, rows, :] = u[1]
            return carry

        lax.fori_loop(0, 4, body, 0)

    def stage2(j, transposed, hooks, put):
        def body(m, carry):
            for n, hook in enumerate(hooks):
                pl.when(m == n)(hook)
            cut = pl.ds(pl.multiple_of(m * HALF, HALF), HALF)
            total = None
            for k in range(2):
                if transposed:
                    a = (lh[2 * j + k, :, cut], ll[2 * j + k, :, cut])
                else:
                    a = (lh[2 * j + k, cut, :], ll[2 * j + k, cut, :])
                t = dot3(a, (uh[k], ul[k]), TN if transposed else NN)
                total = t if total is None else total + t
            put(m, total.reshape(2, RING, SLAB, M))
            return carry

        lax.fori_loop(0, 2, body, 0)

    def put_to(blk):
        def put(m, v):
            Pb[blk, pl.ds(2 * m, 2)] = v

        return put

    def add_to(blk):
        def put(m, v):
            s = pl.ds(2 * m, 2)
            Pb[blk, s] = Pb[blk, s] + v

        return put

    def put_with_pin(m, v):
        s = pl.ds(2 * m, 2)
        Pb[0, s] = v

        @pl.when((core == 1) | (m == 1 - zl))
        def _():
            Pb[0, s] = Pb[0, s] + pin[s]

    def inner(wblk, pblk):
        def body(i, acc):
            return acc + fold((W[wblk, i] * Pb[pblk, i]).reshape(RING * SLAB, M))

        return lax.fori_loop(0, 4, body, jnp.zeros((8, 128), F32))

    def on(pair, fn):
        def run():
            for g in pair:
                fn(g)

        return run

    def chain(*fns):
        def run():
            for f in fns:
                f()

        return run

    G0, G1, S1, S0 = (g00, g01), (g10, g11), (s10, s11), (s00, s01)
    pl.semaphore_wait(barrier, len(peers))
    step1(G0)
    own[0].wait()
    own[1].wait()
    split_op(0)
    on(G0, lambda g: g.spread(0))()
    split_op(1)
    for o in (1, 3, 2):
        on(G0, lambda g: g.spread(o))()
    split_op(2)
    on(G0, lambda g: g.relay(0))()
    split_op(3)
    on(G0, lambda g: g.relay(1))()
    split_op(4)
    on(G0, lambda g: g.relay(3))()
    split_op(5)
    on(G0, lambda g: g.relay(2))()
    step1(G1)
    split_op(6)
    split_op(7)
    for o in (0, 1, 3, 2):
        on(G0, lambda g: g.finish(o))()

    def none():
        pass

    stage1(
        0, 0, True,
        [
            lambda: on(G1, lambda g: g.spread(0))(),
            lambda: on(G1, lambda g: (g.spread(1), g.spread(3)))(),
            lambda: on(G1, lambda g: g.spread(2))(),
            on(G1, lambda g: (g.relay(0), g.relay(1))),
        ],
    )
    stage2(0, False, [on(G1, lambda g: g.relay(3)), on(G1, lambda g: g.relay(2))], put_to(1))
    for o in range(4):
        on(G1, lambda g: g.finish(o))()
    stage1(1, 1, True, [])
    stage2(1, False, [], put_to(2))
    give()
    wait_bytes(recv.at[ahead_got], W.at[2])
    for c in fetch:
        c.wait()
    pp = fold(wv[0] * wv[0]) + fold(wv[1] * wv[1])
    ps = fold(on_[0] * wv[0] * wv[0]) + fold(on_[1] * wv[1] * wv[1])
    ps = ps + 2.0 * (inner(1, 1) + inner(2, 2))
    t0 = Total(0, (GX, GY, GC))
    t1 = Total(16, (GP, GC))
    t0.put(0, jnp.stack([pp, ps]))
    stage1(2, 1, False, [])

    def send_half(pair, half):
        for s in pair:
            for o in range(4):
                s.first(o, half)

    stage2(
        1, True,
        [lambda: (fold_pair(0), t0.step(0), None)[2], lambda: send_half(S1, 0)],
        add_to(1),
    )
    send_half(S1, 1)
    stage1(
        1, 0, False,
        [
            lambda: fold_pair(1),
            lambda: t0.step(1),
            on(S1, lambda s: (s.relay(0), s.relay(1))),
            on(S1, lambda s: s.relay(2)),
        ],
    )
    take_pin()

    def land(pair, cols):
        for o in cols:
            for s in pair:
                s.land(o)

    stage2(
        0, True,
        [
            on(S1, lambda s: s.relay(3)),
            chain(lambda: send_half(S0, 0), lambda: land(S1, (0, 1))),
        ],
        put_with_pin,
    )
    send_half(S0, 1)
    land(S1, (2, 3))
    on(S1, lambda s: s.last())()
    norm_sq, energy_sum = t0.done()
    energy = energy_sum / norm_sq
    for o in range(4):
        on(S0, lambda s: s.relay(o))()
    land(S0, range(4))
    on(S0, lambda s: s.last())()
    pt = jnp.zeros((8, 128), F32)
    tt = jnp.zeros((8, 128), F32)
    out = []
    for b, pair in ((1, S1), (0, S0)):
        for s in pair:
            h = slice(s.h * HALF, s.h * HALF + HALF)
            w, o_ = wv[b, :, h], on_[b, :, h]
            total = s.result()
            ob[0, b, :, h] = total
            sig = o_ * w + total
            gap = o_ - energy
            first = (sig - energy * w) * gap / jnp.maximum(gap * gap, 1.0)
            ob[1, b, :, h] = first
            pt = pt + fold(w * first)
            tt = tt + fold(first * first)
        out.append(pltpu.make_async_copy(ob.at[0, b], psum_out.at[b], out_sem.at[b]))
        out.append(pltpu.make_async_copy(ob.at[1, b], first_out.at[b], out_sem.at[2 + b]))
    t1.put(0, jnp.stack([pt, tt]))
    for c in out:
        c.start()
    t1.step(0)
    correlation, first_sq = t1.done()
    ratio = correlation / norm_sq
    length_sq = first_sq - correlation * ratio
    ratio_out[...] = jnp.broadcast_to(ratio, (8, M))
    scale_out[...] = jnp.broadcast_to(lax.rsqrt(length_sq / float(8 * M * M) + 1e-06), (8, M))
    for c in out:
        c.wait()
    near28 = rbZ.at[:, pl.ds(1, 7)]
    slabs48 = Pb.at[:, :, :, :, lanes(0)]
    for group, like in enumerate((near28, slabs48, W.at[2], slabs48, near28, pin, red.at[pl.ds(0, 35)])):
        wait_bytes(send.at[group], like)


def solution(mesh):
    finer = Mesh(mesh.devices.reshape(2, 2, 4, 4, 2), AXES)
    block = P(SECTOR, OP, None)
    ops = P(SECTOR, OP, None, None)

    def step(wave, onsite, left, right, coupling):
        vm = pl.BlockSpec(memory_space=pltpu.VMEM)
        anyw = pl.BlockSpec(memory_space=pl.ANY)
        shape = jax.ShapeDtypeStruct((2, ROWS, M), F32)
        psum, first, ratio, scale = pl.pallas_call(
            kernel,
            out_shape=(shape, shape) + (jax.ShapeDtypeStruct((8, M), F32),) * 2,
            in_specs=[anyw, anyw, anyw, anyw, pl.BlockSpec(memory_space=pltpu.SMEM)],
            out_specs=(anyw, anyw, vm, vm),
            scratch_shapes=[
                pltpu.VMEM((4, M, M), BF16),
                pltpu.VMEM((4, M, M), BF16),
                pltpu.VMEM((4, M, M), BF16),
                pltpu.VMEM((4, M, M), BF16),
                pltpu.VMEM((3, M, M), F32),
                pltpu.VMEM((3, RING, RING, SLAB, M), F32),
                pltpu.VMEM((2, M, M), BF16),
                pltpu.VMEM((2, M, M), BF16),
                pltpu.VMEM((3, RING, RING, SLAB, M), F32),
                pltpu.VMEM((RING, RING, SLAB, M), F32),
                pltpu.VMEM((2, RING, SLAB, M), F32),
                pltpu.VMEM((4, 4, 3, SLAB, HALF), F32),
                pltpu.VMEM((4, 8, ROWS, HALF), F32),
                pltpu.VMEM((40, 2, 8, 128), F32),
                pltpu.VMEM((2, ROWS, M), F32),
                pltpu.VMEM((2, ROWS, M), F32),
                pltpu.VMEM((2, 2, ROWS, M), F32),
                pltpu.SemaphoreType.DMA((3,)),
                pltpu.SemaphoreType.DMA((2,)),
                pltpu.SemaphoreType.DMA((2,)),
                pltpu.SemaphoreType.DMA((4,)),
                pltpu.SemaphoreType.DMA((N_SEND,)),
                pltpu.SemaphoreType.DMA((N_RECV,)),
            ],
            compiler_params=pltpu.CompilerParams(
                collective_id=0, has_side_effects=True, vmem_limit_bytes=67043328
            ),
        )(wave, onsite, left, right, coupling)
        sigma = onsite * wave + psum
        tiles = (2, ROWS // 8, 8, M)
        second = (first.reshape(tiles) - ratio * wave.reshape(tiles)) * scale
        return sigma, second.reshape(wave.shape)

    return jax.shard_map(
        step,
        mesh=finer,
        in_specs=(block, block, ops, ops, P(SECTOR, OP)),
        out_specs=(block, block),
        check_vma=False,
    )
```

time: 154 us -> 122 us (0.79)
  Pallas kernels: 150 us -> 118 us
  local copies, waits for them, and re-layouts: 3.16 us -> 0.77 us
  other arithmetic: 0 us -> 1.88 us
    pallas_call x1, Pallas kernels: 150 us -> 118 us  [step(): pl.pallas_call(kernel, out_shape=(shape, shape) + (jax.ShapeDtypeStruct((...]
    unnamed x2 -> x0, local copies, waits for them, and re-layouts: 3.16 us -> none
    mul x0 -> x1, other arithmetic: none -> 1.88 us  [step(): second = (first.reshape(tiles) - ratio * wave.reshape(tiles)) * scale]
where the time goes in v2:
time: 122 us
  Pallas kernels  118 us (97%)
  other arithmetic  1.88 us (2%)
    pallas_call x1, Pallas kernels, step(): pl.pallas_call(kernel, out_shape=(shape, shape) + (jax.ShapeDtypeStruct((...  118 us

profile of v2, /device:TPU:1, one launch (start us, length us, event | category | flops | bytes accessed | tf_op | source)
XLA Modules:
  0.0 121.8 jit_solution(12389914083626618406)
XLA Ops:
  0.6 118.5 %shard_map.68 = (f32[2,24,768]{2,1,0:T(8,128)}, f32[2,24,768]{2,1,0:T(8,128)}, f32[8,768]{1,0:T(8,128)}, f32[8,768]{1,0:T(8,128)}) custom-call(f32[2,24,768]{2,1,0:T(8,128)} %wave.1, f32[2,24,768]{2,1,0:T(8,128)} %onsite.1, f32[2,2,768,768]{3,2,1,0:T(8,128)} %left.1, f32[2,2,768,768]{3,2,1,0:T(8,128)} %right.1, s32[2,2]{1,0:T(2,128)} %coup.1), custom_call_target="tpu_custom_call" | custom-call | tf_op jit(solution)/shard_map/pallas_call | solution.py:646
  119.1 0.8 broadcast_bitcast_fusion
  119.9 1.9 %subtract_multiply_fusion = (f32[2,24,768]{2,1,0:T(8,128)}, f32[2,24,768]{2,1,0:T(8,128)}) fusion(f32[2,24,768]{2,1,0:T(8,128)} %get-tuple-element.7, f32[2,24,768]{2,1,0:T(8,128)} %wave.1, f32[24,768]{1,0:T(8,128)S(1)} %get-tuple-element.12, f32[24,768]{1,0:T(8,128)S(1)} %get-tuple-element.13, f32[2,24,768]{2,1,0:T(8,128)} %get-tuple-element.6, ...), kind=kLoop, calls=%fused_computation | loop fusion | flops 184320 | bytes 1032192 | tf_op jit(solution)/shard_map/mul | solution.py:682

commit v3 on v2

--- a/solution.py
+++ b/solution.py
@@ -20,7 +20,7 @@
 ROWS = 24
 HALF = 384
 N_SEND = 7
-N_RECV = 112
+N_RECV = 120
 
 
 def split(v):
@@ -141,7 +141,7 @@
         )
         own[-1].start()
 
-    order = [4, 5, 0, 1, 6, 7, 2, 3]
+    order = [6, 7, 2, 3, 4, 5, 0, 1]
     loads = []
     for n, i in enumerate(order):
         src = left if i < 4 else right
@@ -186,7 +186,8 @@
     def rows_of(z):
         return pl.ds(pl.multiple_of(z * ROWS, 8), ROWS)
 
-    ahead_got = net.new_recv()
+    hand = net.new(lambda: wave.at[0], lambda: W.at[2, x, y, rows_of(zl), :], prev_dev, 0)
+    first_z = jnp.where(core == 1, 1 - zl, zl)
 
     class Gather:
         def __init__(self, blk, h):
@@ -201,70 +202,43 @@
                 px, py = spot(h, pa, pb)
                 return at(px=px, py=py, pz=z)
 
-            self.near, self.got = {}, []
-            for i in range(4):
-                self.got.append(net.new_recv())
-                for o in (1, 0):
-                    if (i, o) != (0, 0):
-                        self.near[i, o] = net.new(
-                            lambda: wave.at[blk, :, lanes(h)],
-                            lambda: W.at[blk, x, y, rows_of(zl), lanes(h)],
-                            dev(mod(a + i), b, (zl + o) % 2),
-                            0,
-                            self.got[i],
-                        )
+            z = first_z if blk == 2 else zl
+            self.z = net.new(
+                (lambda: W.at[2, x, y, rows_of(z), lanes(h)]) if blk == 2 else (lambda: wave.at[blk, :, lanes(h)]),
+                lambda: W.at[blk, x, y, rows_of(z), lanes(h)],
+                at(pz=1 - zl),
+                0,
+            )
+            mine = slab(a, b)
+            self.near = [None] + [net.new(mine, mine, dev(mod(a + i), b), 1) for i in (1, 2, 3)]
             fb, bb = dev(a, mod(b + d)), dev(a, mod(b - d))
-            self.cols, self.ahead = [], []
+            self.cols = []
             for o in range(4):
                 pa = mod(a - o)
                 s, t = slab(pa, b), slab(pa, mod(b - d))
-                self.cols.append((net.new(s, s, fb, 1), net.new(s, s, bb, 1), net.new(t, t, fb, 1)))
-                if blk == 0:
-                    on = []
-                    for pb in (b, mod(b - d), mod(b + d), mod(b + 2)):
-                        px, py = spot(h, pa, pb)
-
-                        def src(px=px, py=py):
-                            return W.at[0, px, py, :, lanes(h)]
-
-                        def dst(px=px, py=py):
-                            return W.at[2, px, py, :, lanes(h)]
-
-                        on.append(net.new(src, dst, prev_dev, 2, ahead_got))
-                    self.ahead.append(on)
-
-        def pass_on(self, o, s):
-            if self.blk == 0:
-                self.ahead[o][s].start()
+                both = net.new_recv()
+                self.cols.append((net.new(s, s, fb, 2), net.new(s, s, bb, 2, both), net.new(t, t, fb, 2, both), both))
 
         def spread(self, o):
             if o == 0:
-                self.near[0, 1].wait_recv()
+                self.z.wait_recv()
+                for i in (1, 3, 2):
+                    self.near[i].start()
             else:
-                wait_bytes(recv.at[self.got[o]], rbB.at[0, 0, 0])
+                self.near[o].wait_recv()
             self.cols[o][0].start()
             self.cols[o][1].start()
-            self.pass_on(o, 0)
 
         def relay(self, o):
             self.cols[o][0].wait_recv()
             self.cols[o][2].start()
-            self.pass_on(o, 1)
 
         def finish(self, o):
-            self.cols[o][1].wait_recv()
-            self.pass_on(o, 2)
-            self.cols[o][2].wait_recv()
-            self.pass_on(o, 3)
-
-    g10, g11, g00, g01 = Gather(1, 0), Gather(1, 1), Gather(0, 0), Gather(0, 1)
-
-    def step1(pair):
-        for i in (0, 1, 3, 2):
-            for o in (1, 0):
-                if (i, o) != (0, 0):
-                    for g in pair:
-                        g.near[i, o].start()
+            wait_bytes(recv.at[self.cols[o][3]], rbB.at[0, 0, pl.ds(0, 2)])
+
+    G1 = Gather(1, 0), Gather(1, 1)
+    G0 = Gather(0, 0), Gather(0, 1)
+    G2 = Gather(2, 0), Gather(2, 1)
 
     class Scatter:
         def __init__(self, blk, h):
@@ -301,26 +275,28 @@
                     )
                 )
             self.near, self.got = [], net.new_recv()
-            for i in (2, 1, 3, 0):
-                for o in (1, 0):
-                    if (i, o) != (0, 0):
-                        px, py = spot(h, mod(a + i), b)
-                        z = (zl + o) % 2
-
-                        def src(px=px, py=py, z=z):
-                            return Pb.at[blk, px, py, rows_of(z), lanes(h)]
-
-                        def dst(k=i * 2 + o):
-                            return rbZ.at[u, k]
-
-                        self.near.append(net.new(src, dst, dev(mod(a + i), b, z), 4, self.got))
-
-        def first(self, o, half=None):
+            for o in range(4):
+                px, py = spot(h, o, b)
+                for k in (1, 0):
+                    z = (zl + k) % 2
+
+                    def src(px=px, py=py, z=z):
+                        return Pb.at[blk, px, py, rows_of(z), lanes(h)]
+
+                    def dst(k=k):
+                        return rbZ.at[u, a * 2 + k]
+
+                    self.near.append(
+                        net.new(src, dst, dev(o, b, z), 4, self.got, sends=None if k else a != o)
+                    )
+
+        def first(self, o, half):
             c = self.cols[o]
-            if half is None or self.h == 0:
-                if half is None or o // 2 == half:
-                    c[0].start()
-                    c[1].start()
+            if half is None or (self.h == 0 and o // 2 == half):
+                c[0].start()
+                c[1].start()
+            elif self.h == 0:
+                pass
             else:
                 pl.when(lax.div(mod(self.b + 2), 2) == half)(c[0].start)
                 pl.when(lax.div(mod(self.b - d), 2) == half)(c[1].start)
@@ -337,19 +313,19 @@
             wait_bytes(recv.at[c[3]], rbB.at[self.u, o, pl.ds(1, 2)])
             s = self.slab(o, self.b)()
             s[...] = s[...] + self.rb(o, 1)[...] + self.rb(o, 2)[...]
-
-        def last(self):
-            for c in self.near:
-                c.start()
+            self.near[2 * o].start()
+            self.near[2 * o + 1].start()
 
         def result(self):
             wait_bytes(recv.at[self.got], rbZ.at[self.u, pl.ds(1, 7)])
-            t = Pb[self.blk, x, y, rows_of(zl), lanes(self.h)]
+            rbZ[self.u, self.a * 2] = Pb[self.blk, x, y, rows_of(zl), lanes(self.h)]
+            t = rbZ[self.u, 0]
             for k in range(1, 8):
                 t = t + rbZ[self.u, k]
             return t
 
-    s10, s11, s00, s01 = Scatter(1, 0), Scatter(1, 1), Scatter(0, 0), Scatter(0, 1)
+    S1 = Scatter(1, 0), Scatter(1, 1)
+    S0 = Scatter(0, 0), Scatter(0, 1)
 
     ex = [
         net.new((lambda q=q: Pb.at[2, (1 - zl) * 2 + q]), (lambda q=q: zin.at[q]), at(pz=1 - zl), 5, sends=core == 1)
@@ -357,7 +333,7 @@
     ]
     pin_got = net.new_recv()
     far = [
-        net.new((lambda q=q: Pb.at[2, zl * 2 + q]), (lambda q=q: pin.at[zl * 2 + q]), next_dev, 5, pin_got)
+        net.new((lambda q=q: zin.at[q]), (lambda q=q: pin.at[zl * 2 + q]), next_dev, 5, pin_got)
         for q in range(2)
     ]
     chip = [
@@ -365,20 +341,31 @@
         for q in range(4)
     ]
 
-    def take_pin():
-        pl.when(core == 1)(lambda: wait_bytes(recv.at[pin_got], pin))
-        pl.when(core == 0)(lambda: wait_bytes(recv.at[pin_got], pin.at[pl.ds(0, 2)]))
-
-    def give():
-        for c in ex + chip:
+    def take_pin(c):
+        @pl.when(core == c)
+        def _():
+            n = 4 if c else 2
+            wait_bytes(recv.at[pin_got], pin.at[pl.ds(0, n)])
+
+            def add(i, carry):
+                k = i if c else (1 - zl) * 2 + i
+                Pb[0, k] = Pb[0, k] + pin[k]
+                return carry
+
+            lax.fori_loop(0, n, add, 0)
+            for u in S0:
+                for o in range(4):
+                    u.first(o, None)
+
+    def give(first):
+        for c in ex if first else chip:
             c.start()
 
     def fold_pair(q):
         @pl.when(core == 1)
         def _():
             ex[q].desc().wait_recv()
-            i = zl * 2 + q
-            Pb[2, i] = Pb[2, i] + zin[q]
+            zin[q] = zin[q] + Pb[2, zl * 2 + q]
             far[q].desc().start()
 
     plane = []
@@ -428,7 +415,7 @@
             s = self.get(len(self.stages) - 1)
             return jnp.sum(s[0], keepdims=True), jnp.sum(s[1], keepdims=True)
 
-    def stage1(blk, j, transposed, hooks):
+    def stage1(blk, j, transposed, hooks, at_u=0):
         def body(i, carry):
             for n, hook in enumerate(hooks):
                 pl.when(i == n)(hook)
@@ -438,50 +425,41 @@
             r = (rh[2 * j + k], rl[2 * j + k])
             u = split(dot3(w, r, NT if transposed else NN))
             rows = pl.ds(pl.multiple_of(m * HALF, HALF), HALF)
-            uh[k, rows, :] = u[0]
-            ul[k, rows, :] = u[1]
+            uh[at_u + k, rows, :] = u[0]
+            ul[at_u + k, rows, :] = u[1]
             return carry
 
         lax.fori_loop(0, 4, body, 0)
 
-    def stage2(j, transposed, hooks, put):
-        def body(m, carry):
-            for n, hook in enumerate(hooks):
-                pl.when(m == n)(hook)
+    def stage2(parts, hooks, put, flip=None):
+        def body(i, carry):
+            m = i if flip is None else jnp.where(flip, 1 - i, i)
             cut = pl.ds(pl.multiple_of(m * HALF, HALF), HALF)
             total = None
-            for k in range(2):
-                if transposed:
-                    a = (lh[2 * j + k, :, cut], ll[2 * j + k, :, cut])
-                else:
-                    a = (lh[2 * j + k, cut, :], ll[2 * j + k, cut, :])
-                t = dot3(a, (uh[k], ul[k]), TN if transposed else NN)
-                total = t if total is None else total + t
+            for n, hook in enumerate(hooks):
+                if hook is not none:
+                    pl.when(i == n)(hook)
+            for j, transposed, at_u in parts:
+                for k in range(2):
+                    if transposed:
+                        a = (lh[2 * j + k, :, cut], ll[2 * j + k, :, cut])
+                    else:
+                        a = (lh[2 * j + k, cut, :], ll[2 * j + k, cut, :])
+                    t = dot3(a, (uh[at_u + k], ul[at_u + k]), TN if transposed else NN)
+                    total = t if total is None else total + t
             put(m, total.reshape(2, RING, SLAB, M))
             return carry
 
         lax.fori_loop(0, 2, body, 0)
+
+    def none():
+        pass
 
     def put_to(blk):
         def put(m, v):
             Pb[blk, pl.ds(2 * m, 2)] = v
 
         return put
-
-    def add_to(blk):
-        def put(m, v):
-            s = pl.ds(2 * m, 2)
-            Pb[blk, s] = Pb[blk, s] + v
-
-        return put
-
-    def put_with_pin(m, v):
-        s = pl.ds(2 * m, 2)
-        Pb[0, s] = v
-
-        @pl.when((core == 1) | (m == 1 - zl))
-        def _():
-            Pb[0, s] = Pb[0, s] + pin[s]
 
     def inner(wblk, pblk):
         def body(i, acc):
@@ -496,114 +474,110 @@
 
         return run
 
-    def chain(*fns):
+    def send_half(pair, half):
+        for s in pair:
+            for o in range(4):
+                s.first(o, half)
+
+    def land(pair, cols):
+        for o in cols:
+            for s in pair:
+                s.land(o)
+
+    def do(*acts):
         def run():
-            for f in fns:
-                f()
+            for a in acts:
+                a()
 
         return run
 
-    G0, G1, S1, S0 = (g00, g01), (g10, g11), (s10, s11), (s00, s01)
+    def spread(pair, *cols):
+        return lambda: [on(pair, lambda g: g.spread(o))() for o in cols] and None
+
+    def relay(pair, *cols):
+        return lambda: [on(pair, lambda g: g.relay(o))() for o in cols] and None
+
+    def finish(pair, *cols):
+        return lambda: [on(pair, lambda g: g.finish(o))() for o in cols] and None
+
     pl.semaphore_wait(barrier, len(peers))
-    step1(G0)
+    for g in G1:
+        g.z.start()
+    hand.start()
+    for g in G0:
+        g.z.start()
     own[0].wait()
     own[1].wait()
     split_op(0)
-    on(G0, lambda g: g.spread(0))()
+    spread(G1, 0)()
     split_op(1)
-    for o in (1, 3, 2):
-        on(G0, lambda g: g.spread(o))()
     split_op(2)
-    on(G0, lambda g: g.relay(0))()
+    spread(G1, 1, 3)()
     split_op(3)
-    on(G0, lambda g: g.relay(1))()
+    spread(G1, 2)()
     split_op(4)
-    on(G0, lambda g: g.relay(3))()
+    hand.wait_recv()
+    for g in G2:
+        g.z.start()
+    relay(G1, 0)()
     split_op(5)
-    on(G0, lambda g: g.relay(2))()
-    step1(G1)
+    relay(G1, 1)()
     split_op(6)
+    relay(G1, 3)()
     split_op(7)
-    for o in (0, 1, 3, 2):
-        on(G0, lambda g: g.finish(o))()
-
-    def none():
-        pass
-
+    relay(G1, 2)()
+    spread(G0, 0)()
+    finish(G1, 0, 1, 3, 2)()
+    stage1(1, 1, True, [none, spread(G0, 1, 3), spread(G0, 2), relay(G0, 0)])
+    stage2(
+        [(1, False, 0)],
+        [relay(G0, 1, 3), do(lambda: give(True), relay(G0, 2))],
+        put_to(2),
+        zl == 0,
+    )
+    give(False)
     stage1(
-        0, 0, True,
-        [
-            lambda: on(G1, lambda g: g.spread(0))(),
-            lambda: on(G1, lambda g: (g.spread(1), g.spread(3)))(),
-            lambda: on(G1, lambda g: g.spread(2))(),
-            on(G1, lambda g: (g.relay(0), g.relay(1))),
-        ],
+        1, 0, False,
+        [do(finish(G0, 0, 1), spread(G2, 0)), finish(G0, 3, 2), none, spread(G2, 1, 3)],
     )
-    stage2(0, False, [on(G1, lambda g: g.relay(3)), on(G1, lambda g: g.relay(2))], put_to(1))
-    for o in range(4):
-        on(G1, lambda g: g.finish(o))()
-    stage1(1, 1, True, [])
-    stage2(1, False, [], put_to(2))
-    give()
-    wait_bytes(recv.at[ahead_got], W.at[2])
+    stage2([(0, True, 0)], [do(lambda: fold_pair(0), spread(G2, 2)), relay(G2, 0)], put_to(0))
     for c in fetch:
         c.wait()
     pp = fold(wv[0] * wv[0]) + fold(wv[1] * wv[1])
     ps = fold(on_[0] * wv[0] * wv[0]) + fold(on_[1] * wv[1] * wv[1])
-    ps = ps + 2.0 * (inner(1, 1) + inner(2, 2))
+    ps = ps + 2.0 * inner(0, 0)
+    fold_pair(1)
+    take_pin(1)
+    stage1(0, 0, True, [relay(G2, 1), relay(G2, 3), relay(G2, 2)])
+    finish(G2, 0, 1, 3, 2)()
+    ps = ps + 2.0 * inner(2, 2)
     t0 = Total(0, (GX, GY, GC))
     t1 = Total(16, (GP, GC))
     t0.put(0, jnp.stack([pp, ps]))
-    stage1(2, 1, False, [])
-
-    def send_half(pair, half):
-        for s in pair:
-            for o in range(4):
-                s.first(o, half)
-
+
+    def early(*acts):
+        return lambda: pl.when(core == 1)(do(*acts))
+
+    def late(*acts):
+        return lambda: pl.when(core == 0)(do(*acts))
+
+    stage1(2, 1, False, [none, early(relay(S0, 0, 1, 2, 3)), lambda: take_pin(0)], 2)
     stage2(
-        1, True,
-        [lambda: (fold_pair(0), t0.step(0), None)[2], lambda: send_half(S1, 0)],
-        add_to(1),
+        [(0, False, 0), (1, True, 2)],
+        [
+            do(lambda: t0.step(0), early(lambda: land(S0, range(4)))),
+            do(lambda: send_half(S1, 0), lambda: t0.step(1), late(relay(S0, 0, 1, 2, 3))),
+        ],
+        put_to(1),
     )
     send_half(S1, 1)
-    stage1(
-        1, 0, False,
-        [
-            lambda: fold_pair(1),
-            lambda: t0.step(1),
-            on(S1, lambda s: (s.relay(0), s.relay(1))),
-            on(S1, lambda s: s.relay(2)),
-        ],
-    )
-    take_pin()
-
-    def land(pair, cols):
-        for o in cols:
-            for s in pair:
-                s.land(o)
-
-    stage2(
-        0, True,
-        [
-            on(S1, lambda s: s.relay(3)),
-            chain(lambda: send_half(S0, 0), lambda: land(S1, (0, 1))),
-        ],
-        put_with_pin,
-    )
-    send_half(S0, 1)
-    land(S1, (2, 3))
-    on(S1, lambda s: s.last())()
+    relay(S1[:1], 0, 1)()
+    late(lambda: land(S0, range(4)))()
     norm_sq, energy_sum = t0.done()
     energy = energy_sum / norm_sq
-    for o in range(4):
-        on(S0, lambda s: s.relay(o))()
-    land(S0, range(4))
-    on(S0, lambda s: s.last())()
-    pt = jnp.zeros((8, 128), F32)
-    tt = jnp.zeros((8, 128), F32)
     out = []
-    for b, pair in ((1, S1), (0, S0)):
+
+    def close(b, pair, pt, tt):
         for s in pair:
             h = slice(s.h * HALF, s.h * HALF + HALF)
             w, o_ = wv[b, :, h], on_[b, :, h]
@@ -617,6 +591,16 @@
             tt = tt + fold(first * first)
         out.append(pltpu.make_async_copy(ob.at[0, b], psum_out.at[b], out_sem.at[b]))
         out.append(pltpu.make_async_copy(ob.at[1, b], first_out.at[b], out_sem.at[2 + b]))
+        return pt, tt
+
+    relay(S1[1:], 0, 1, 2, 3)()
+    relay(S1[:1], 2, 3)()
+    land(S1[:1], (0, 1))
+    land(S1[1:], (0, 1, 2, 3))
+    land(S1[:1], (2, 3))
+    zero = jnp.zeros((8, 128), F32)
+    pt, tt = close(0, S0, zero, zero)
+    pt, tt = close(1, S1, pt, tt)
     t1.put(0, jnp.stack([pt, tt]))
     for c in out:
         c.start()
@@ -624,13 +608,21 @@
     correlation, first_sq = t1.done()
     ratio = correlation / norm_sq
     length_sq = first_sq - correlation * ratio
-    ratio_out[...] = jnp.broadcast_to(ratio, (8, M))
-    scale_out[...] = jnp.broadcast_to(lax.rsqrt(length_sq / float(8 * M * M) + 1e-06), (8, M))
+    ratio_out[...] = jnp.broadcast_to(ratio, (ROWS, M))
+    scale_out[...] = jnp.broadcast_to(lax.rsqrt(length_sq / float(8 * M * M) + 1e-06), (ROWS, M))
     for c in out:
         c.wait()
-    near28 = rbZ.at[:, pl.ds(1, 7)]
-    slabs48 = Pb.at[:, :, :, :, lanes(0)]
-    for group, like in enumerate((near28, slabs48, W.at[2], slabs48, near28, pin, red.at[pl.ds(0, 35)])):
+    slabs = Pb.at[:, :, :, :, lanes(0)]
+    waits = (
+        rbZ.at[0],
+        rbB.at[pl.ds(0, 3), pl.ds(0, 2)],
+        Pb.at[:, :, pl.ds(0, 3)],
+        slabs,
+        rbZ.at[:, pl.ds(1, 7)],
+        pin,
+        red.at[pl.ds(0, 35)],
+    )
+    for group, like in enumerate(waits):
         wait_bytes(send.at[group], like)
 
 
@@ -645,7 +637,7 @@
         shape = jax.ShapeDtypeStruct((2, ROWS, M), F32)
         psum, first, ratio, scale = pl.pallas_call(
             kernel,
-            out_shape=(shape, shape) + (jax.ShapeDtypeStruct((8, M), F32),) * 2,
+            out_shape=(shape, shape) + (jax.ShapeDtypeStruct((ROWS, M), F32),) * 2,
             in_specs=[anyw, anyw, anyw, anyw, pl.BlockSpec(memory_space=pltpu.SMEM)],
             out_specs=(anyw, anyw, vm, vm),
             scratch_shapes=[
@@ -655,8 +647,8 @@
                 pltpu.VMEM((4, M, M), BF16),
                 pltpu.VMEM((3, M, M), F32),
                 pltpu.VMEM((3, RING, RING, SLAB, M), F32),
-                pltpu.VMEM((2, M, M), BF16),
-                pltpu.VMEM((2, M, M), BF16),
+                pltpu.VMEM((4, M, M), BF16),
+                pltpu.VMEM((4, M, M), BF16),
                 pltpu.VMEM((3, RING, RING, SLAB, M), F32),
                 pltpu.VMEM((RING, RING, SLAB, M), F32),
                 pltpu.VMEM((2, RING, SLAB, M), F32),
@@ -678,9 +670,7 @@
             ),
         )(wave, onsite, left, right, coupling)
         sigma = onsite * wave + psum
-        tiles = (2, ROWS // 8, 8, M)
-        second = (first.reshape(tiles) - ratio * wave.reshape(tiles)) * scale
-        return sigma, second.reshape(wave.shape)
+        return sigma, (first - ratio * wave) * scale
 
     return jax.shard_map(
         step,

time: 122 us -> 117 us (0.959)
  Pallas kernels: 118 us -> 114 us
    pallas_call x1, Pallas kernels: 118 us -> 114 us  [step(): pl.pallas_call(kernel, out_shape=(shape, shape) + (jax.ShapeDtypeStruct((...]
where the time goes in v3:
time: 117 us
  Pallas kernels  114 us (97%)
  other arithmetic  1.96 us (2%)
    pallas_call x1, Pallas kernels, step(): pl.pallas_call(kernel, out_shape=(shape, shape) + (jax.ShapeDtypeStruct((...  114 us

profile of v3, /device:TPU:1, one launch (start us, length us, event | category | flops | bytes accessed | tf_op | source)
XLA Modules:
  0.0 116.7 jit_solution(4120362797594512959)
XLA Ops:
  0.6 114.1 %shard_map.68 = (f32[2,24,768]{2,1,0:T(8,128)}, f32[2,24,768]{2,1,0:T(8,128)}, f32[24,768]{1,0:T(8,128)}, f32[24,768]{1,0:T(8,128)}) custom-call(f32[2,24,768]{2,1,0:T(8,128)} %wave.1, f32[2,24,768]{2,1,0:T(8,128)} %onsite.1, f32[2,2,768,768]{3,2,1,0:T(8,128)} %left.1, f32[2,2,768,768]{3,2,1,0:T(8,128)} %right.1, s32[2,2]{1,0:T(2,128)} %coup.1), custom_call_target="tpu_custom_call" | custom-call | tf_op jit(solution)/shard_map/pallas_call | solution.py:638
  114.7 2.0 %subtract_multiply_fusion = (f32[2,24,768]{2,1,0:T(8,128)}, f32[2,24,768]{2,1,0:T(8,128)}) fusion(f32[2,24,768]{2,1,0:T(8,128)} %get-tuple-element.7, f32[2,24,768]{2,1,0:T(8,128)} %wave.1, f32[24,768]{1,0:T(8,128)} %get-tuple-element.9, f32[24,768]{1,0:T(8,128)} %get-tuple-element.8, f32[2,24,768]{2,1,0:T(8,128)} %get-tuple-element.6, f32[2,24,768]{2,1,0:T(8,128)} %onsite.1), kind=kLoop, calls=%fused_computation | loop fusion | flops 184320 | bytes 1032192 | tf_op jit(solution)/shard_map/mul | solution.py:673

commit v4 on v3

--- a/solution.py
+++ b/solution.py
@@ -430,6 +430,19 @@
             return carry
 
         lax.fori_loop(0, 4, body, 0)
+
+    def stage1_at(px, at_u, hooks=()):
+        def body(k, carry):
+            for n, hook in enumerate(hooks):
+                pl.when(k == n)(hook)
+            w = split(W[1, px].reshape(RING * SLAB, M))
+            u = split(dot3(w, (rh[k], rl[k]), NN))
+            rows = pl.ds(pl.multiple_of(px * RING * SLAB, RING * SLAB), RING * SLAB)
+            uh[at_u + k, rows, :] = u[0]
+            ul[at_u + k, rows, :] = u[1]
+            return carry
+
+        lax.fori_loop(0, 2, body, 0)
 
     def stage2(parts, hooks, put, flip=None):
         def body(i, carry):
@@ -527,7 +540,12 @@
     split_op(7)
     relay(G1, 2)()
     spread(G0, 0)()
-    finish(G1, 0, 1, 3, 2)()
+    finish(G1[:1], 0)()
+    stage1_at(x, 2)
+    finish(G1[:1], 1, 3)()
+    stage1_at(mod(x - d), 2)
+    finish(G1[:1], 2)()
+    finish(G1[1:], 0, 1, 2, 3)()
     stage1(1, 1, True, [none, spread(G0, 1, 3), spread(G0, 2), relay(G0, 0)])
     stage2(
         [(1, False, 0)],
@@ -536,19 +554,16 @@
         zl == 0,
     )
     give(False)
-    stage1(
-        1, 0, False,
-        [do(finish(G0, 0, 1), spread(G2, 0)), finish(G0, 3, 2), none, spread(G2, 1, 3)],
-    )
-    stage2([(0, True, 0)], [do(lambda: fold_pair(0), spread(G2, 2)), relay(G2, 0)], put_to(0))
+    stage1_at(mod(x + d), 2, [none, do(finish(G0, 0, 1), spread(G2, 0))])
+    stage1_at(mod(x + 2), 2, [none, finish(G0, 3, 2)])
+    stage2([(0, True, 2)], [spread(G2, 1, 3), do(lambda: fold_pair(0), spread(G2, 2))], put_to(0))
     for c in fetch:
         c.wait()
     pp = fold(wv[0] * wv[0]) + fold(wv[1] * wv[1])
     ps = fold(on_[0] * wv[0] * wv[0]) + fold(on_[1] * wv[1] * wv[1])
     ps = ps + 2.0 * inner(0, 0)
-    fold_pair(1)
     take_pin(1)
-    stage1(0, 0, True, [relay(G2, 1), relay(G2, 3), relay(G2, 2)])
+    stage1(0, 0, True, [relay(G2, 0), do(relay(G2, 1), lambda: fold_pair(1)), relay(G2, 3), relay(G2, 2)])
     finish(G2, 0, 1, 3, 2)()
     ps = ps + 2.0 * inner(2, 2)
     t0 = Total(0, (GX, GY, GC))

time: 117 us -> 117 us (level)
  no operation moved by 1% of the time
where the time goes in v4:
time: 117 us
  Pallas kernels  114 us (97%)
  other arithmetic  1.96 us (2%)
    pallas_call x1, Pallas kernels, step(): pl.pallas_call(kernel, out_shape=(shape, shape) + (jax.ShapeDtypeStruct((...  114 us

profile of v4, /device:TPU:1, one launch (start us, length us, event | category | flops | bytes accessed | tf_op | source)
XLA Modules:
  0.0 117.0 jit_solution(16549813691906177169)
XLA Ops:
  0.6 114.4 %shard_map.68 = (f32[2,24,768]{2,1,0:T(8,128)}, f32[2,24,768]{2,1,0:T(8,128)}, f32[24,768]{1,0:T(8,128)}, f32[24,768]{1,0:T(8,128)}) custom-call(f32[2,24,768]{2,1,0:T(8,128)} %wave.1, f32[2,24,768]{2,1,0:T(8,128)} %onsite.1, f32[2,2,768,768]{3,2,1,0:T(8,128)} %left.1, f32[2,2,768,768]{3,2,1,0:T(8,128)} %right.1, s32[2,2]{1,0:T(2,128)} %coup.1), custom_call_target="tpu_custom_call" | custom-call | tf_op jit(solution)/shard_map/pallas_call | solution.py:653
  115.1 2.0 %subtract_multiply_fusion = (f32[2,24,768]{2,1,0:T(8,128)}, f32[2,24,768]{2,1,0:T(8,128)}) fusion(f32[2,24,768]{2,1,0:T(8,128)} %get-tuple-element.7, f32[2,24,768]{2,1,0:T(8,128)} %wave.1, f32[24,768]{1,0:T(8,128)} %get-tuple-element.9, f32[24,768]{1,0:T(8,128)} %get-tuple-element.8, f32[2,24,768]{2,1,0:T(8,128)} %get-tuple-element.6, f32[2,24,768]{2,1,0:T(8,128)} %onsite.1), kind=kLoop, calls=%fused_computation | loop fusion | flops 184320 | bytes 1032192 | tf_op jit(solution)/shard_map/mul | solution.py:688
